TPU v7x, 128 devices: a whole 4x4x4 slice. The times are simulated.
128 devices in a mesh: dp: 32 (over x, z, core), mp: 4 (over y).
Axes of the slice: x: 4, y: 4, z: 4, core: 2. Of those that a mesh axis runs over, the one named last changes fastest.
Arguments:
- tokens: bfloat16 [8192, 1024], P('dp', 'mp'), may hold values from -6 to 6
- grad_out: bfloat16 [8192, 1024], P('dp', 'mp'), may hold values from -6 to 6
- gates: bfloat16 [8192, 2], P('dp'), may hold values from 0.099609375 to 0.8984375
- expert_ids: int32 [8192, 2], P('dp'), may hold values from 0 to 63, all different within a row; in each aligned block of 256 rows (0 to 255, 256 to 511, ...) at most 16 rows name the same one
- w_gate: bfloat16 [64, 1024, 4096], P('dp', None, 'mp'), may hold values from -0.1875 to 0.1875
- w_up: bfloat16 [64, 1024, 4096], P('dp', None, 'mp'), may hold values from -0.1875 to 0.1875
- w_down: bfloat16 [64, 4096, 1024], P('dp', 'mp'), may hold values from -0.09375 to 0.09375
Outputs:
- grad_tokens: bfloat16 [8192, 1024], P('dp', 'mp')
- grad_gates: float32 [8192, 2], P('dp')
- grad_w_gate: bfloat16 [64, 1024, 4096], P('dp', None, 'mp')
- grad_w_up: bfloat16 [64, 1024, 4096], P('dp', None, 'mp')
- grad_w_down: bfloat16 [64, 4096, 1024], P('dp', 'mp')
Inputs may be any that keep to these rules, and one draw needn't show every extreme that they name: `expert_ids`: among the 256 tokens of one index of dp no expert is named more than 16 times, and in some such block some expert is named exactly 16 times; the two experts of a token differ.
All inputs are finite; a program needn't handle non-finite values.
Results may differ from a plain program's by a relative error of at most 0.0058.
Values may be sent and summed in bfloat16 or wider, within the bound.
A program may use at most 128 MiB of HBM per device.

v0:
```python
import jax
import jax.numpy as jnp
from jax import lax
from jax.sharding import PartitionSpec as P


def on_device(tokens, grad_out, gates, expert_ids, w_gate, w_up, w_down):
    count_tokens = tokens.shape[0]
    width_share = tokens.shape[1]
    groups = lax.axis_size("dp")
    local_experts = w_gate.shape[0]
    width_full = w_down.shape[2]
    all_experts = local_experts * groups
    capacity = max(2, 4 * count_tokens // all_experts)
    total_slots = all_experts * capacity
    onehot = (
        expert_ids[:, :, None] == jnp.arange(all_experts, dtype=jnp.int32)[None, None, :]
    ).astype(jnp.int32)
    onehot = onehot.reshape(count_tokens * 2, all_experts)
    before = jnp.cumsum(onehot, axis=0) - onehot
    position = jnp.sum(before * onehot, axis=1)
    slot_of = expert_ids.reshape(-1) * capacity + position
    placed = slot_of[None, :] == jnp.arange(total_slots, dtype=jnp.int32)[:, None]
    placed = placed.astype(jnp.bfloat16).reshape(total_slots, count_tokens, 2)
    route = jnp.sum(placed.astype(jnp.float32), axis=2).astype(jnp.bfloat16)
    slot_gate = jnp.einsum("stk,tk->s", placed, gates, preferred_element_type=jnp.float32).astype(
        jnp.bfloat16
    )
    slot_gate = slot_gate.reshape(groups, local_experts * capacity)
    full_x, full_dy = (
        lax.all_gather(tokens, "mp", axis=1, tiled=True),
        lax.all_gather(grad_out, "mp", axis=1, tiled=True),
    )
    send_x = jnp.dot(route, full_x, preferred_element_type=jnp.float32).astype(jnp.bfloat16)
    send_dy = jnp.dot(route, full_dy, preferred_element_type=jnp.float32).astype(jnp.bfloat16)
    send_x = send_x.reshape(groups, local_experts * capacity, width_full)
    send_dy = send_dy.reshape(groups, local_experts * capacity, width_full)
    recv_x, recv_dy, recv_gate = (
        lax.all_to_all(send_x, "dp", split_axis=0, concat_axis=0, tiled=True),
        lax.all_to_all(send_dy, "dp", split_axis=0, concat_axis=0, tiled=True),
        lax.all_to_all(slot_gate, "dp", split_axis=0, concat_axis=0, tiled=True),
    )
    recv_x = recv_x.reshape(groups, local_experts, capacity, width_full)
    recv_dy = recv_dy.reshape(groups, local_experts, capacity, width_full)
    recv_gate = recv_gate.reshape(groups, local_experts, capacity)
    grads_gate = []
    grads_up = []
    grads_down = []
    input_parts = []
    gate_parts = []
    for expert in range(local_experts):
        rows_x = recv_x[:, expert]
        rows_dy = recv_dy[:, expert]
        rows_gate = recv_gate[:, expert]
        gate_pre = jnp.einsum(
            "scd,df->scf", rows_x, w_gate[expert], preferred_element_type=jnp.float32
        )
        up_pre = jnp.einsum("scd,df->scf", rows_x, w_up[expert], preferred_element_type=jnp.float32)
        sigmoid_gate = jax.nn.sigmoid(gate_pre)
        activated = gate_pre * sigmoid_gate
        hidden = (activated * up_pre).astype(jnp.bfloat16)
        output_part = jnp.einsum(
            "scf,fd->scd", hidden, w_down[expert], preferred_element_type=jnp.float32
        )
        gate_parts.append(jnp.sum(rows_dy.astype(jnp.float32) * output_part, axis=2))
        scaled = (rows_gate.astype(jnp.float32)[:, :, None] * rows_dy.astype(jnp.float32)).astype(
            jnp.bfloat16
        )
        hidden_grad = jnp.einsum(
            "scd,fd->scf", scaled, w_down[expert], preferred_element_type=jnp.float32
        )
        dgate = (
            hidden_grad * up_pre * sigmoid_gate * (1.0 + gate_pre * (1.0 - sigmoid_gate))
        ).astype(jnp.bfloat16)
        dup = (hidden_grad * activated).astype(jnp.bfloat16)
        grads_down.append(
            jnp.einsum("scf,scd->fd", hidden, scaled, preferred_element_type=jnp.float32).astype(
                jnp.bfloat16
            )
        )
        grads_gate.append(
            jnp.einsum("scd,scf->df", rows_x, dgate, preferred_element_type=jnp.float32).astype(
                jnp.bfloat16
            )
        )
        grads_up.append(
            jnp.einsum("scd,scf->df", rows_x, dup, preferred_element_type=jnp.float32).astype(
                jnp.bfloat16
            )
        )
        input_parts.append(
            jnp.einsum("scf,df->scd", dgate, w_gate[expert], preferred_element_type=jnp.float32)
            + jnp.einsum("scf,df->scd", dup, w_up[expert], preferred_element_type=jnp.float32)
        )
    gate_stack = jnp.stack(gate_parts, axis=1)
    input_stack = jnp.stack(input_parts, axis=1)
    gate_total = lax.psum(gate_stack, "mp")
    back_gates = lax.all_to_all(gate_total, "dp", split_axis=0, concat_axis=0, tiled=True)
    back_gates = back_gates.reshape(total_slots)
    grad_gates = jnp.take(back_gates, slot_of, axis=0).reshape(count_tokens, 2)
    input_share = lax.psum_scatter(input_stack, "mp", scatter_dimension=3, tiled=True)
    back_rows = lax.all_to_all(input_share, "dp", split_axis=0, concat_axis=0, tiled=True)
    back_rows = back_rows.reshape(total_slots, width_share)
    picked = jnp.take(back_rows, slot_of, axis=0).reshape(count_tokens, 2, width_share)
    grad_tokens = jnp.sum(picked, axis=1).astype(jnp.bfloat16)
    return (
        grad_tokens,
        grad_gates,
        jnp.stack(grads_gate, axis=0),
        jnp.stack(grads_up, axis=0),
        jnp.stack(grads_down, axis=0),
    )


def solution(mesh):
    placed = (
        P("dp", "mp"),
        P("dp", "mp"),
        P("dp", None),
        P("dp", None),
        P("dp", None, "mp"),
        P("dp", None, "mp"),
        P("dp", "mp", None),
    )
    return jax.shard_map(
        on_device,
        mesh=mesh,
        in_specs=placed,
        out_specs=(
            P("dp", "mp"),
            P("dp", None),
            P("dp", None, "mp"),
            P("dp", None, "mp"),
            P("dp", "mp", None),
        ),
        check_vma=False,
    )
```

profile of v0, /device:TPU:1, one launch (start us, length us, event | category | flops | bytes accessed | tf_op | source)
XLA Modules:
  0.0 213.9 jit_solution(18338866497481159757)
XLA Ops:
  11.4 9.4 %all-to-all-start = ((bf16[32,1,32]{2,1,0:T(2,128)(2,1)}), bf16[32,1,32]{2,1,0:T(2,128)(2,1)S(1)}, u32[]{:S(2)}, u32[]{:S(2)}) async-start(bf16[32,1,32]{2,1,0:T(2,128)(2,1)} %all_to_all.24), calls=%async_computation | async-start | bytes 32768 | tf_op jit(solution)/shard_map/all_to_all | solution.py:41
  21.3 11.1 %all_gather.7 = bf16[256,1024]{1,0:T(8,128)(2,1)S(1)} all-gather(bf16[256,256]{1,0:T(8,128)(2,1)S(1)} %copy-done.9), channel_id=1, replica_groups=mesh['dp'=32,'mp'=4] {'mp'}, dimensions={1}, use_global_device_ids=true | all-gather | bytes 655360 | tf_op jit(solution)/shard_map/all_gather | solution.py:31
  34.5 9.7 %all-to-all-start.2 = ((bf16[32,32,1024]{2,1,0:T(8,128)(2,1)}), bf16[32,32,1024]{2,1,0:T(8,128)(2,1)S(1)}, u32[]{:S(2)}, u32[]{:S(2)}) async-start(bf16[32,32,1024]{2,1,0:T(8,128)(2,1)} %bitcast.10), calls=%async_computation.2 | async-start | bytes 4194304 | tf_op jit(solution)/shard_map/all_to_all | solution.py:39
  44.2 11.5 %all_gather.6 = bf16[256,1024]{1,0:T(8,128)(2,1)S(1)} all-gather(bf16[256,256]{1,0:T(8,128)(2,1)S(1)} %copy-done.10), channel_id=1, replica_groups=mesh['dp'=32,'mp'=4] {'mp'}, dimensions={1}, use_global_device_ids=true | all-gather | bytes 655360 | tf_op jit(solution)/shard_map/all_gather | solution.py:32
  57.8 14.8 %all-to-all-done.2 = bf16[32,32,1024]{2,1,0:T(8,128)(2,1)S(1)} async-done(((bf16[32,32,1024]{2,1,0:T(8,128)(2,1)}), bf16[32,32,1024]{2,1,0:T(8,128)(2,1)S(1)}, u32[]{:S(2)}, u32[]{:S(2)}) %all-to-all-start.2) | async-done | bytes 2097184 | tf_op jit(solution)/shard_map/all_to_all | solution.py:39
  72.5 5.2 %all-to-all-start.1 = ((bf16[32,32,1024]{2,1,0:T(8,128)(2,1)}), bf16[32,32,1024]{2,1,0:T(8,128)(2,1)}, u32[]{:S(2)}, u32[]{:S(2)}) async-start(bf16[32,32,1024]{2,1,0:T(8,128)(2,1)} %bitcast.5), calls=%async_computation.1 | async-start | bytes 4194304 | tf_op jit(solution)/shard_map/all_to_all | solution.py:40
  78.9 4.3 %fusion.12 = f32[32,16,1024]{2,1,0:T(8,128)} fusion(bf16[2,1024,1024]{2,1,0:T(8,128)(2,1)} %param.11, bf16[32,2,16,1024]{3,2,1,0:T(8,128)(2,1)S(1)} %bitcast.215), kind=kOutput, calls=%fused_computation.28 | convolution fusion | flops 1073741824 | bytes 5242880 | tf_op jit(solution)/shard_map/scd,df->scf/dot_general | solution.py:55
  83.3 2.6 %fusion.24 = f32[32,16,1024]{2,1,0:T(8,128)} fusion(bf16[2,1024,1024]{2,1,0:T(8,128)(2,1)S(1)} %copy-done.12, bf16[32,2,16,1024]{3,2,1,0:T(8,128)(2,1)S(1)} %bitcast.216), kind=kOutput, calls=%fused_computation.40 | convolution fusion | flops 1073741824 | bytes 5242880 | tf_op jit(solution)/shard_map/scd,df->scf/dot_general | solution.py:55
  85.8 20.3 %all-to-all-done.1 = bf16[32,32,1024]{2,1,0:T(8,128)(2,1)} async-done(((bf16[32,32,1024]{2,1,0:T(8,128)(2,1)}), bf16[32,32,1024]{2,1,0:T(8,128)(2,1)}, u32[]{:S(2)}, u32[]{:S(2)}) %all-to-all-start.1) | async-done | bytes 2097184 | tf_op jit(solution)/shard_map/all_to_all | solution.py:40
  106.2 3.4 %fusion.20 = f32[32,16,1024]{2,1,0:T(8,128)S(1)} fusion(bf16[2,1024,1024]{2,1,0:T(8,128)(2,1)} %param.13, f32[32,16]{1,0:T(8,128)S(1)} %copy.79, bf16[32,2,16,1024]{3,2,1,0:T(8,128)(2,1)} %bitcast.6), kind=kOutput, calls=%fused_computation.36 | convolution fusion | flops 1075314688 | bytes 5244928 | tf_op jit(solution)/shard_map/scd,fd->scf/dot_general | solution.py:69
  110.0 3.0 %multiply_convert_fusion = (bf16[32,16,1024]{2,1,0:T(8,128)(2,1)}, bf16[32,16,1024]{2,1,0:T(8,128)(2,1)S(1)}, bf16[32,16,1024]{2,1,0:T(8,128)(2,1)S(1)}) fusion(f32[32,16,1024]{2,1,0:T(8,128)S(1)} %copy-done.19, f32[32,16,1024]{2,1,0:T(8,128)S(1)} %fusion.20, bf16[2,1024,1024]{2,1,0:T(8,128)(2,1)S(1)} %copy-done.14, bf16[32,2,16,1024]{3,2,1,0:T(8,128)(2,1)S(1)} %bitcast.217), kind=kOutput, calls=%fused_computation.50 | convolution fusion | flops 1081606144 | bytes 10485760 | tf_op jit(solution)/shard_map/scd,df->scf/dot_general | solution.py:58
  116.2 2.7 %fusion.32 = f32[32,16,1024]{2,1,0:T(8,128)S(1)} fusion(bf16[2,1024,1024]{2,1,0:T(8,128)(2,1)S(1)} %copy-done.15, f32[32,16]{1,0:T(8,128)S(1)} %copy.76, bf16[32,2,16,1024]{3,2,1,0:T(8,128)(2,1)} %bitcast.6), kind=kOutput, calls=%fused_computation.48 | convolution fusion | flops 1075314688 | bytes 5259264 | tf_op jit(solution)/shard_map/scd,fd->scf/dot_general | solution.py:69
  118.9 3.0 %multiply_convert_fusion.1 = (bf16[32,16,1024]{2,1,0:T(8,128)(2,1)}, bf16[32,16,1024]{2,1,0:T(8,128)(2,1)S(1)}, bf16[32,16,1024]{2,1,0:T(8,128)(2,1)S(1)}) fusion(f32[32,16,1024]{2,1,0:T(8,128)S(1)} %copy-done.18, f32[32,16,1024]{2,1,0:T(8,128)S(1)} %fusion.32, bf16[2,1024,1024]{2,1,0:T(8,128)(2,1)S(1)} %copy-done.14, ...), kind=kOutput, calls=%fused_computation.51 | convolution fusion | flops 1081606144 | bytes 10485760 | tf_op jit(solution)/shard_map/scd,df->scf/dot_general | solution.py:58
  128.6 3.7 %fusion.7 = f32[32,16]{1,0:T(8,128)S(1)} fusion(bf16[32,16,1024]{2,1,0:T(8,128)(2,1)} %get-tuple-element.25, bf16[2,1024,1024]{2,1,0:T(8,128)(2,1)} %param.13, bf16[32,2,16,1024]{3,2,1,0:T(8,128)(2,1)} %bitcast.6), kind=kOutput, calls=%fused_computation.23 | convolution fusion | flops 1075314176 | bytes 4196352 | tf_op jit(solution)/shard_map/scf,fd->scd/dot_general | solution.py:62
  135.0 17.0 %psum.7 = f32[32,2,16]{2,1,0:T(2,128)} all-reduce(f32[32,2,16]{2,1,0:T(2,128)S(1)} %pad_maximum_fusion.4), channel_id=1, replica_groups=mesh['dp'=32,'mp'=4] {'mp'}, use_global_device_ids=true, to_apply=%region_8.9 | all-reduce | flops 1024 | bytes 8192 | tf_op jit(solution)/shard_map/psum | solution.py:97
  151.9 7.1 %all-to-all-start.4 = ((f32[32,2,16]{2,1,0:T(2,128)}), f32[32,2,16]{2,1,0:T(2,128)}, u32[]{:S(2)}, u32[]{:S(2)}) async-start(f32[32,2,16]{2,1,0:T(2,128)} %psum.7), calls=%async_computation.5 | async-start | bytes 65536 | tf_op jit(solution)/shard_map/all_to_all | solution.py:98
  159.0 4.0 %fusion.51 = bf16[1,1024,1024]{2,1,0:T(8,128)(2,1)} fusion(bf16[32,16,1024]{2,1,0:T(8,128)(2,1)} %copy-done.20, bf16[32,2,16,1024]{3,2,1,0:T(8,128)(2,1)S(1)} %bitcast.219), kind=kOutput, calls=%fused_computation.80 | convolution fusion | flops 1074790400 | bytes 4194304 | tf_op jit(solution)/shard_map/scd,scf->df/dot_general | solution.py:82
  163.0 2.6 %fusion.50 = bf16[1,1024,1024]{2,1,0:T(8,128)(2,1)} fusion(bf16[32,16,1024]{2,1,0:T(8,128)(2,1)S(1)} %copy-done.22, bf16[32,2,16,1024]{3,2,1,0:T(8,128)(2,1)S(1)} %bitcast.220), kind=kOutput, calls=%fused_computation.79 | convolution fusion | flops 1074790400 | bytes 4194304 | tf_op jit(solution)/shard_map/scd,scf->df/dot_general | solution.py:82
  165.7 4.0 %fusion.55 = bf16[1,1024,1024]{2,1,0:T(8,128)(2,1)} fusion(bf16[32,16,1024]{2,1,0:T(8,128)(2,1)S(1)} %copy-done.23, f32[32,16]{1,0:T(8,128)S(1)} %copy.79, bf16[32,2,16,1024]{3,2,1,0:T(8,128)(2,1)} %bitcast.6), kind=kOutput, calls=%fused_computation.84 | convolution fusion | flops 1076363264 | bytes 4196352 | tf_op jit(solution)/shard_map/scf,scd->fd/dot_general | solution.py:77
  169.7 3.9 %fusion.54 = bf16[1,1024,1024]{2,1,0:T(8,128)(2,1)} fusion(bf16[32,16,1024]{2,1,0:T(8,128)(2,1)S(1)} %copy-done.25, f32[32,16]{1,0:T(8,128)S(1)} %copy.76, bf16[32,2,16,1024]{3,2,1,0:T(8,128)(2,1)} %bitcast.6), kind=kOutput, calls=%fused_computation.83 | convolution fusion | flops 1076363264 | bytes 4196352 | tf_op jit(solution)/shard_map/scf,scd->fd/dot_general | solution.py:77
  173.6 2.6 %fusion.53 = bf16[1,1024,1024]{2,1,0:T(8,128)(2,1)} fusion(bf16[32,16,1024]{2,1,0:T(8,128)(2,1)S(1)} %get-tuple-element.27, bf16[32,2,16,1024]{3,2,1,0:T(8,128)(2,1)S(1)} %bitcast.221), kind=kOutput, calls=%fused_computation.82 | convolution fusion | flops 1074790400 | bytes 4194304 | tf_op jit(solution)/shard_map/scd,scf->df/dot_general | solution.py:87
  178.6 7.5 %all-to-all-start.3 = ((f32[32,2,16,256]{3,2,1,0:T(8,128)}), f32[32,2,16,256]{3,2,1,0:T(8,128)S(1)}, u32[]{:S(2)}, u32[]{:S(2)}) async-start(f32[32,2,16,256]{3,2,1,0:T(8,128)} %copy.82), calls=%async_computation.4 | async-start | bytes 2097152 | tf_op jit(solution)/shard_map/all_to_all | solution.py:102
  186.1 2.7 %fusion.52 = bf16[1,1024,1024]{2,1,0:T(8,128)(2,1)S(1)} fusion(bf16[32,16,1024]{2,1,0:T(8,128)(2,1)} %copy-done.17, bf16[32,2,16,1024]{3,2,1,0:T(8,128)(2,1)S(1)} %bitcast.222), kind=kOutput, calls=%fused_computation.81 | convolution fusion | flops 1074790400 | bytes 4194304 | tf_op jit(solution)/shard_map/scd,scf->df/dot_general | solution.py:87
  193.2 3.7 %pad_maximum_fusion.1 = (bf16[2,1024,1024]{2,1,0:T(8,128)(2,1)}, bf16[2,1024,1024]{2,1,0:T(8,128)(2,1)}) fusion(bf16[1,1024,1024]{2,1,0:T(8,128)(2,1)S(1)} %copy-done.4, bf16[1,1024,1024]{2,1,0:T(8,128)(2,1)S(1)} %copy-done.5, bf16[1,1024,1024]{2,1,0:T(8,128)(2,1)S(1)} %copy-done.6, bf16[1,1024,1024]{2,1,0:T(8,128)(2,1)S(1)} %fusion.52), kind=kLoop, calls=%fused_computation.3 | loop fusion | flops 4194304 | bytes 16777216 | tf_op jit(solution)/shard_map/stack | solution.py:109
  (100 shorter events, 39.7 us)
Async XLA Ops:
  7.2 3.1 %copy-start = (bf16[256,2]{0,1:T(2,128)(2,1)S(1)}, bf16[256,2]{0,1:T(2,128)(2,1)}, u32[]{:S(2)}) copy-start(bf16[256,2]{0,1:T(2,128)(2,1)} %param.9) | copy-start | bytes 3076
  7.2 14.1 %copy-start.9 = (bf16[256,256]{1,0:T(8,128)(2,1)S(1)}, bf16[256,256]{1,0:T(8,128)(2,1)}, u32[]{:S(2)}) copy-start(bf16[256,256]{1,0:T(8,128)(2,1)} %param.7) | copy-start | bytes 393220
  11.4 23.0 %all-to-all-start = ((bf16[32,1,32]{2,1,0:T(2,128)(2,1)}), bf16[32,1,32]{2,1,0:T(2,128)(2,1)S(1)}, u32[]{:S(2)}, u32[]{:S(2)}) async-start(bf16[32,1,32]{2,1,0:T(2,128)(2,1)} %all_to_all.24), calls=%async_computation | async-start | bytes 32768 | tf_op jit(solution)/shard_map/all_to_all | solution.py:41
  34.4 9.7 %copy-start.10 = (bf16[256,256]{1,0:T(8,128)(2,1)S(1)}, bf16[256,256]{1,0:T(8,128)(2,1)}, u32[]{:S(2)}) copy-start(bf16[256,256]{1,0:T(8,128)(2,1)} %param.8) | copy-start | bytes 393220
  34.5 38.1 %all-to-all-start.2 = ((bf16[32,32,1024]{2,1,0:T(8,128)(2,1)}), bf16[32,32,1024]{2,1,0:T(8,128)(2,1)S(1)}, u32[]{:S(2)}, u32[]{:S(2)}) async-start(bf16[32,32,1024]{2,1,0:T(8,128)(2,1)} %bitcast.10), calls=%async_computation.2 | async-start | bytes 4194304 | tf_op jit(solution)/shard_map/all_to_all | solution.py:39
  72.5 33.6 %all-to-all-start.1 = ((bf16[32,32,1024]{2,1,0:T(8,128)(2,1)}), bf16[32,32,1024]{2,1,0:T(8,128)(2,1)}, u32[]{:S(2)}, u32[]{:S(2)}) async-start(bf16[32,32,1024]{2,1,0:T(8,128)(2,1)} %bitcast.5), calls=%async_computation.1 | async-start | bytes 4194304 | tf_op jit(solution)/shard_map/all_to_all | solution.py:40
  77.7 98.5 %reduce-scatter.2.cloned.1.call-start = ((), (), s32[]{:S(2)}) async-start(), calls=%async_computation.6 | async-start | bytes 5242880 | tf_op jit(solution)/shard_map/reduce_scatter | solution.py:101
  78.9 4.3 %copy-start.12 = (bf16[2,1024,1024]{2,1,0:T(8,128)(2,1)S(1)}, bf16[2,1024,1024]{2,1,0:T(8,128)(2,1)}, u32[]{:S(2)}) copy-start(bf16[2,1024,1024]{2,1,0:T(8,128)(2,1)} %param.11) | copy-start | bytes 12582916
  106.2 3.4 %copy-start.14 = (bf16[2,1024,1024]{2,1,0:T(8,128)(2,1)S(1)}, bf16[2,1024,1024]{2,1,0:T(8,128)(2,1)}, u32[]{:S(2)}) copy-start(bf16[2,1024,1024]{2,1,0:T(8,128)(2,1)} %param.12) | copy-start | bytes 12582916
  106.2 3.8 %copy-start.19 = (f32[32,16,1024]{2,1,0:T(8,128)S(1)}, f32[32,16,1024]{2,1,0:T(8,128)}, u32[]{:S(2)}) copy-start(f32[32,16,1024]{2,1,0:T(8,128)} %fusion.12) | copy-start | bytes 6291460
  110.0 4.0 %copy-start.13 = (bf16[2,1024,1024]{2,1,0:T(8,128)(2,1)S(1)}, bf16[2,1024,1024]{2,1,0:T(8,128)(2,1)}, u32[]{:S(2)}) copy-start(bf16[2,1024,1024]{2,1,0:T(8,128)(2,1)} %param.11) | copy-start | bytes 12582916
  128.6 3.7 %copy-start.16 = (bf16[2,1024,1024]{2,1,0:T(8,128)(2,1)S(1)}, bf16[2,1024,1024]{2,1,0:T(8,128)(2,1)}, u32[]{:S(2)}) copy-start(bf16[2,1024,1024]{2,1,0:T(8,128)(2,1)} %param.13) | copy-start | bytes 12582916
  128.6 3.7 %copy-start.24 = (bf16[32,16,1024]{2,1,0:T(8,128)(2,1)S(1)}, bf16[32,16,1024]{2,1,0:T(8,128)(2,1)}, u32[]{:S(2)}) copy-start(bf16[32,16,1024]{2,1,0:T(8,128)(2,1)} %get-tuple-element.22) | copy-start | bytes 3145732
  151.9 26.7 %all-to-all-start.4 = ((f32[32,2,16]{2,1,0:T(2,128)}), f32[32,2,16]{2,1,0:T(2,128)}, u32[]{:S(2)}, u32[]{:S(2)}) async-start(f32[32,2,16]{2,1,0:T(2,128)} %psum.7), calls=%async_computation.5 | async-start | bytes 65536 | tf_op jit(solution)/shard_map/all_to_all | solution.py:98
  159.0 4.0 %copy-start.22 = (bf16[32,16,1024]{2,1,0:T(8,128)(2,1)S(1)}, bf16[32,16,1024]{2,1,0:T(8,128)(2,1)}, u32[]{:S(2)}) copy-start(bf16[32,16,1024]{2,1,0:T(8,128)(2,1)} %copy-done.21) | copy-start | bytes 3145732
  165.7 4.0 %copy-start.25 = (bf16[32,16,1024]{2,1,0:T(8,128)(2,1)S(1)}, bf16[32,16,1024]{2,1,0:T(8,128)(2,1)}, u32[]{:S(2)}) copy-start(bf16[32,16,1024]{2,1,0:T(8,128)(2,1)} %get-tuple-element.22) | copy-start | bytes 3145732
  178.6 24.4 %all-to-all-start.3 = ((f32[32,2,16,256]{3,2,1,0:T(8,128)}), f32[32,2,16,256]{3,2,1,0:T(8,128)S(1)}, u32[]{:S(2)}, u32[]{:S(2)}) async-start(f32[32,2,16,256]{3,2,1,0:T(8,128)} %copy.82), calls=%async_computation.4 | async-start | bytes 2097152 | tf_op jit(solution)/shard_map/all_to_all | solution.py:102
  186.1 2.7 %copy-start.2 = (bf16[1,1024,1024]{2,1,0:T(8,128)(2,1)S(1)}, bf16[1,1024,1024]{2,1,0:T(8,128)(2,1)}, u32[]{:S(2)}) copy-start(bf16[1,1024,1024]{2,1,0:T(8,128)(2,1)} %fusion.55) | copy-start | bytes 6291460
  186.1 2.7 %copy-start.3 = (bf16[1,1024,1024]{2,1,0:T(8,128)(2,1)S(1)}, bf16[1,1024,1024]{2,1,0:T(8,128)(2,1)}, u32[]{:S(2)}) copy-start(bf16[1,1024,1024]{2,1,0:T(8,128)(2,1)} %fusion.54) | copy-start | bytes 6291460
  188.8 3.7 %copy-start.5 = (bf16[1,1024,1024]{2,1,0:T(8,128)(2,1)S(1)}, bf16[1,1024,1024]{2,1,0:T(8,128)(2,1)}, u32[]{:S(2)}) copy-start(bf16[1,1024,1024]{2,1,0:T(8,128)(2,1)} %fusion.50) | copy-start | bytes 6291460
  188.9 4.4 %copy-start.6 = (bf16[1,1024,1024]{2,1,0:T(8,128)(2,1)S(1)}, bf16[1,1024,1024]{2,1,0:T(8,128)(2,1)}, u32[]{:S(2)}) copy-start(bf16[1,1024,1024]{2,1,0:T(8,128)(2,1)} %fusion.53) | copy-start | bytes 6291460
  193.2 4.6 %copy-start.11 = (s32[1024]{0:T(1024)S(1)}, s32[1024]{0:T(1024)}, u32[]{:S(2)}) copy-start(s32[1024]{0:T(1024)} %pad_clamp_fusion) | copy-start | bytes 12292
  196.9 3.3 %copy-start.8 = (s32[256,2]{1,0:T(8,128)S(1)}, s32[256,2]{1,0:T(8,128)}, u32[]{:S(2)}) copy-start(s32[256,2]{1,0:T(8,128)} %copy-done.7) | copy-start | bytes 6148
  203.0 4.0 %copy-start.1 = (bf16[256,2]{0,1:T(2,128)(2,1)S(1)}, bf16[256,2]{0,1:T(2,128)(2,1)}, u32[]{:S(2)}) copy-start(bf16[256,2]{0,1:T(2,128)(2,1)} %param.9) | copy-start | bytes 3076
  (8 other events, 16.2 us)
Sparse Core Ops, SparseCore 0:
  128.7 44.9 reduce-scatter.1
where the time goes:
time: 215 us; the launch traced here: 214 us
  matrix products  55 us (26%)
  blocking collectives  39.6 us (18%)
  starting transfers between devices  39.1 us (18%)
  waiting for transfers between devices  37.1 us (17%)
  local copies, waits for them, and re-layouts  15.2 us (7%)
  between operations  14.4 us (7%)
  other arithmetic  13.4 us (6%)
    all_to_all x1, waiting for transfers between devices, on_device(): lax.all_to_all(send_dy, 'dp', split_axis=0, concat_axis=0, tiled=True)  20.3 us
    psum x1, blocking collectives, on_device(): gate_total = lax.psum(gate_stack, 'mp')  17 us
    all_to_all x1, waiting for transfers between devices, on_device(): lax.all_to_all(send_x, 'dp', split_axis=0, concat_axis=0, tiled=True)  14.8 us
    all_gather x1, blocking collectives, on_device(): lax.all_gather(grad_out, 'mp', axis=1, tiled=True)  11.5 us
    all_gather x1, blocking collectives, on_device(): lax.all_gather(tokens, 'mp', axis=1, tiled=True)  11.1 us
    all_to_all x1, starting transfers between devices, on_device(): lax.all_to_all(send_x, 'dp', split_axis=0, concat_axis=0, tiled=True)  9.72 us
    all_to_all x1, starting transfers between devices, on_device(): lax.all_to_all(slot_gate, 'dp', split_axis=0, concat_axis=0, tiled=True)  9.42 us
    dot_general x2, matrix products, on_device(): jnp.einsum('scf,scd->fd', hidden, scaled, preferred_element_type=jnp.floa...  7.93 us
  transfers between devices with their start and end apart: 6, of which 3 were waited for; matrix products, arithmetic and copies ran while one was open for 24% of the time, Pallas kernels for 0%

commit v1 on v0

--- a/solution.py
+++ b/solution.py
@@ -2,6 +2,14 @@
 import jax.numpy as jnp
 from jax import lax
 from jax.sharding import PartitionSpec as P
+
+
+def add_in_pairs(x, axis):
+    size, total = (lax.axis_size(axis), x)
+    for far in [1 << k for k in range(size.bit_length() - 1)]:
+        route = [(i, i ^ far) for i in range(size)]
+        total = total + lax.ppermute(total, axis, route)
+    return total
 
 
 def on_device(tokens, grad_out, gates, expert_ids, w_gate, w_up, w_down):
@@ -94,7 +102,7 @@
         )
     gate_stack = jnp.stack(gate_parts, axis=1)
     input_stack = jnp.stack(input_parts, axis=1)
-    gate_total = lax.psum(gate_stack, "mp")
+    gate_total = add_in_pairs(gate_stack, "mp")
     back_gates = lax.all_to_all(gate_total, "dp", split_axis=0, concat_axis=0, tiled=True)
     back_gates = back_gates.reshape(total_slots)
     grad_gates = jnp.take(back_gates, slot_of, axis=0).reshape(count_tokens, 2)

time: 215 us -> 212 us (0.986)
  blocking collectives: 39.6 us -> 22.6 us
  waiting for transfers between devices: 37.1 us -> 50.2 us
  starting transfers between devices: 39.1 us -> 42.3 us
    psum x1 -> x0, blocking collectives: 17 us -> none  [on_device(): gate_total = lax.psum(gate_stack, 'mp')]
    reduce_scatter x1, waiting for transfers between devices: 0.01 us -> 12.2 us  [on_device(): lax.psum_scatter(input_stack, 'mp', scatter_dimension=3, tiled=True)]
    ppermute x0 -> x2, starting transfers between devices: none -> 4.24 us  [add_in_pairs(): total = total + lax.ppermute(total, axis, route)]
  transfers between devices with their start and end apart: 6 -> 8, of which waited for: 3 -> 4; matrix products, arithmetic and copies ran while one was open for 24% -> 24% of each run, Pallas kernels for 0% -> 0%
where the time goes in v1:
time: 212 us; the launch traced here: 211 us
  matrix products  53.6 us (25%)
  waiting for transfers between devices  50.2 us (24%)
  starting transfers between devices  42.3 us (20%)
  blocking collectives  22.6 us (11%)
  between operations  14.4 us (7%)
  other arithmetic  14.1 us (7%)
  local copies, waits for them, and re-layouts  13.8 us (7%)
    all_to_all x1, waiting for transfers between devices, on_device(): lax.all_to_all(send_dy, 'dp', split_axis=0, concat_axis=0, tiled=True)  20.3 us
    all_to_all x1, waiting for transfers between devices, on_device(): lax.all_to_all(send_x, 'dp', split_axis=0, concat_axis=0, tiled=True)  14.8 us
    reduce_scatter x1, waiting for transfers between devices, on_device(): lax.psum_scatter(input_stack, 'mp', scatter_dimension=3, tiled=True)  12.2 us
    all_gather x1, blocking collectives, on_device(): lax.all_gather(grad_out, 'mp', axis=1, tiled=True)  11.5 us
    all_gather x1, blocking collectives, on_device(): lax.all_gather(tokens, 'mp', axis=1, tiled=True)  11.1 us
    all_to_all x1, starting transfers between devices, on_device(): lax.all_to_all(send_x, 'dp', split_axis=0, concat_axis=0, tiled=True)  9.72 us
    all_to_all x1, starting transfers between devices, on_device(): lax.all_to_all(slot_gate, 'dp', split_axis=0, concat_axis=0, tiled=True)  9.42 us
    dot_general x2, matrix products, on_device(): jnp.einsum('scf,scd->fd', hidden, scaled, preferred_element_type=jnp.floa...  7.82 us
  transfers between devices with their start and end apart: 8, of which 4 were waited for; matrix products, arithmetic and copies ran while one was open for 24% of the time, Pallas kernels for 0%

profile of v1, /device:TPU:1, one launch (start us, length us, event | category | flops | bytes accessed | tf_op | source)
XLA Modules:
  0.0 211.1 jit_solution(3256262611984160011)
XLA Ops:
  11.4 9.4 %all-to-all-start = ((bf16[32,1,32]{2,1,0:T(2,128)(2,1)}), bf16[32,1,32]{2,1,0:T(2,128)(2,1)S(1)}, u32[]{:S(2)}, u32[]{:S(2)}) async-start(bf16[32,1,32]{2,1,0:T(2,128)(2,1)} %all_to_all.24), calls=%async_computation | async-start | bytes 32768 | tf_op jit(solution)/shard_map/all_to_all | solution.py:49
  21.3 11.1 %all_gather.7 = bf16[256,1024]{1,0:T(8,128)(2,1)S(1)} all-gather(bf16[256,256]{1,0:T(8,128)(2,1)S(1)} %copy-done.9), channel_id=1, replica_groups=mesh['dp'=32,'mp'=4] {'mp'}, dimensions={1}, use_global_device_ids=true | all-gather | bytes 655360 | tf_op jit(solution)/shard_map/all_gather | solution.py:39
  34.5 9.7 %all-to-all-start.2 = ((bf16[32,32,1024]{2,1,0:T(8,128)(2,1)}), bf16[32,32,1024]{2,1,0:T(8,128)(2,1)S(1)}, u32[]{:S(2)}, u32[]{:S(2)}) async-start(bf16[32,32,1024]{2,1,0:T(8,128)(2,1)} %bitcast.10), calls=%async_computation.2 | async-start | bytes 4194304 | tf_op jit(solution)/shard_map/all_to_all | solution.py:47
  44.2 11.5 %all_gather.6 = bf16[256,1024]{1,0:T(8,128)(2,1)S(1)} all-gather(bf16[256,256]{1,0:T(8,128)(2,1)S(1)} %copy-done.10), channel_id=1, replica_groups=mesh['dp'=32,'mp'=4] {'mp'}, dimensions={1}, use_global_device_ids=true | all-gather | bytes 655360 | tf_op jit(solution)/shard_map/all_gather | solution.py:40
  57.8 14.8 %all-to-all-done.2 = bf16[32,32,1024]{2,1,0:T(8,128)(2,1)S(1)} async-done(((bf16[32,32,1024]{2,1,0:T(8,128)(2,1)}), bf16[32,32,1024]{2,1,0:T(8,128)(2,1)S(1)}, u32[]{:S(2)}, u32[]{:S(2)}) %all-to-all-start.2) | async-done | bytes 2097184 | tf_op jit(solution)/shard_map/all_to_all | solution.py:47
  72.5 5.2 %all-to-all-start.1 = ((bf16[32,32,1024]{2,1,0:T(8,128)(2,1)}), bf16[32,32,1024]{2,1,0:T(8,128)(2,1)}, u32[]{:S(2)}, u32[]{:S(2)}) async-start(bf16[32,32,1024]{2,1,0:T(8,128)(2,1)} %bitcast.5), calls=%async_computation.1 | async-start | bytes 4194304 | tf_op jit(solution)/shard_map/all_to_all | solution.py:48
  78.9 4.3 %fusion.12 = f32[32,16,1024]{2,1,0:T(8,128)} fusion(bf16[2,1024,1024]{2,1,0:T(8,128)(2,1)} %param.11, bf16[32,2,16,1024]{3,2,1,0:T(8,128)(2,1)S(1)} %bitcast.215), kind=kOutput, calls=%fused_computation.28 | convolution fusion | flops 1073741824 | bytes 5242880 | tf_op jit(solution)/shard_map/scd,df->scf/dot_general | solution.py:63
  85.9 20.3 %all-to-all-done.1 = bf16[32,32,1024]{2,1,0:T(8,128)(2,1)} async-done(((bf16[32,32,1024]{2,1,0:T(8,128)(2,1)}), bf16[32,32,1024]{2,1,0:T(8,128)(2,1)}, u32[]{:S(2)}, u32[]{:S(2)}) %all-to-all-start.1) | async-done | bytes 2097184 | tf_op jit(solution)/shard_map/all_to_all | solution.py:48
  106.2 3.4 %fusion.20 = f32[32,16,1024]{2,1,0:T(8,128)S(1)} fusion(bf16[2,1024,1024]{2,1,0:T(8,128)(2,1)} %param.13, f32[32,16]{1,0:T(8,128)S(1)} %copy.79, bf16[32,2,16,1024]{3,2,1,0:T(8,128)(2,1)} %bitcast.6), kind=kOutput, calls=%fused_computation.36 | convolution fusion | flops 1075314688 | bytes 5244928 | tf_op jit(solution)/shard_map/scd,fd->scf/dot_general | solution.py:77
  110.0 3.0 %multiply_convert_fusion = (bf16[32,16,1024]{2,1,0:T(8,128)(2,1)}, bf16[32,16,1024]{2,1,0:T(8,128)(2,1)S(1)}, bf16[32,16,1024]{2,1,0:T(8,128)(2,1)S(1)}) fusion(f32[32,16,1024]{2,1,0:T(8,128)S(1)} %copy-done.21, f32[32,16,1024]{2,1,0:T(8,128)S(1)} %fusion.20, bf16[2,1024,1024]{2,1,0:T(8,128)(2,1)S(1)} %copy-done.14, bf16[32,2,16,1024]{3,2,1,0:T(8,128)(2,1)S(1)} %bitcast.217), kind=kOutput, calls=%fused_computation.50 | convolution fusion | flops 1081606144 | bytes 10485760 | tf_op jit(solution)/shard_map/scd,df->scf/dot_general | solution.py:66
  115.6 2.7 %fusion.32 = f32[32,16,1024]{2,1,0:T(8,128)S(1)} fusion(bf16[2,1024,1024]{2,1,0:T(8,128)(2,1)S(1)} %copy-done.15, f32[32,16]{1,0:T(8,128)S(1)} %copy.76, bf16[32,2,16,1024]{3,2,1,0:T(8,128)(2,1)} %bitcast.6), kind=kOutput, calls=%fused_computation.48 | convolution fusion | flops 1075314688 | bytes 5259264 | tf_op jit(solution)/shard_map/scd,fd->scf/dot_general | solution.py:77
  118.3 3.0 %multiply_convert_fusion.1 = (bf16[32,16,1024]{2,1,0:T(8,128)(2,1)}, bf16[32,16,1024]{2,1,0:T(8,128)(2,1)S(1)}, bf16[32,16,1024]{2,1,0:T(8,128)(2,1)S(1)}) fusion(f32[32,16,1024]{2,1,0:T(8,128)S(1)} %copy-done.20, f32[32,16,1024]{2,1,0:T(8,128)S(1)} %fusion.32, bf16[2,1024,1024]{2,1,0:T(8,128)(2,1)S(1)} %copy-done.14, ...), kind=kOutput, calls=%fused_computation.51 | convolution fusion | flops 1081606144 | bytes 10485760 | tf_op jit(solution)/shard_map/scd,df->scf/dot_general | solution.py:66
  128.0 3.7 %fusion.7 = f32[32,16]{1,0:T(8,128)S(1)} fusion(bf16[32,16,1024]{2,1,0:T(8,128)(2,1)} %get-tuple-element.25, bf16[2,1024,1024]{2,1,0:T(8,128)(2,1)} %param.13, bf16[32,2,16,1024]{3,2,1,0:T(8,128)(2,1)} %bitcast.6), kind=kOutput, calls=%fused_computation.23 | convolution fusion | flops 1075314176 | bytes 4196352 | tf_op jit(solution)/shard_map/scf,fd->scd/dot_general | solution.py:70
  131.7 2.7 %fusion.4 = f32[32,16]{1,0:T(8,128)S(1)} fusion(bf16[32,16,1024]{2,1,0:T(8,128)(2,1)S(1)} %copy-done.25, bf16[2,1024,1024]{2,1,0:T(8,128)(2,1)S(1)} %copy-done.16, bf16[32,2,16,1024]{3,2,1,0:T(8,128)(2,1)} %bitcast.6), kind=kOutput, calls=%fused_computation.20 | convolution fusion | flops 1075314176 | bytes 4196352 | tf_op jit(solution)/shard_map/scf,fd->scd/dot_general | solution.py:70
  136.2 3.9 %fusion.55 = bf16[1,1024,1024]{2,1,0:T(8,128)(2,1)} fusion(bf16[32,16,1024]{2,1,0:T(8,128)(2,1)S(1)} %copy-done.24, f32[32,16]{1,0:T(8,128)S(1)} %copy.79, bf16[32,2,16,1024]{3,2,1,0:T(8,128)(2,1)} %bitcast.6), kind=kOutput, calls=%fused_computation.84 | convolution fusion | flops 1076363264 | bytes 4196352 | tf_op jit(solution)/shard_map/scf,scd->fd/dot_general | solution.py:85
  140.1 3.9 %fusion.54 = bf16[1,1024,1024]{2,1,0:T(8,128)(2,1)} fusion(bf16[32,16,1024]{2,1,0:T(8,128)(2,1)S(1)} %copy-done.25, f32[32,16]{1,0:T(8,128)S(1)} %copy.76, bf16[32,2,16,1024]{3,2,1,0:T(8,128)(2,1)} %bitcast.6), kind=kOutput, calls=%fused_computation.83 | convolution fusion | flops 1076363264 | bytes 4196352 | tf_op jit(solution)/shard_map/scf,scd->fd/dot_general | solution.py:85
  149.2 2.6 %fusion.50 = bf16[1,1024,1024]{2,1,0:T(8,128)(2,1)} fusion(bf16[32,16,1024]{2,1,0:T(8,128)(2,1)S(1)} %copy-done.23, bf16[32,2,16,1024]{3,2,1,0:T(8,128)(2,1)S(1)} %bitcast.220), kind=kOutput, calls=%fused_computation.79 | convolution fusion | flops 1074790400 | bytes 4194304 | tf_op jit(solution)/shard_map/scd,scf->df/dot_general | solution.py:90
  152.5 5.8 %all-to-all-start.4 = ((f32[32,2,16]{2,1,0:T(2,128)}), f32[32,2,16]{2,1,0:T(2,128)S(1)}, u32[]{:S(2)}, u32[]{:S(2)}) async-start(f32[32,2,16]{2,1,0:T(2,128)} %fusion.101), calls=%async_computation.5 | async-start | bytes 65536 | tf_op jit(solution)/shard_map/all_to_all | solution.py:106
  158.3 2.7 %fusion.53 = bf16[1,1024,1024]{2,1,0:T(8,128)(2,1)} fusion(bf16[32,16,1024]{2,1,0:T(8,128)(2,1)S(1)} %copy-done.19, bf16[32,2,16,1024]{3,2,1,0:T(8,128)(2,1)S(1)} %bitcast.221), kind=kOutput, calls=%fused_computation.82 | convolution fusion | flops 1074790400 | bytes 4194304 | tf_op jit(solution)/shard_map/scd,scf->df/dot_general | solution.py:95
  161.0 12.2 %reduce-scatter.2.cloned.1.call-done = f32[32,2,16,256]{3,2,0,1:T(8,128)} async-done(((f32[32,2,16,1024]{3,2,0,1:T(8,128)}), f32[32,2,16,256]{3,2,0,1:T(8,128)}) %reduce-scatter.2.cloned.1.call-update) | async-done | bytes 1048592 | tf_op jit(solution)/shard_map/reduce_scatter | solution.py:109
  175.6 7.8 %all-to-all-start.3 = ((f32[32,2,16,256]{3,2,1,0:T(8,128)}), f32[32,2,16,256]{3,2,1,0:T(8,128)S(1)}, u32[]{:S(2)}, u32[]{:S(2)}) async-start(f32[32,2,16,256]{3,2,1,0:T(8,128)} %copy.82), calls=%async_computation.4 | async-start | bytes 2097152 | tf_op jit(solution)/shard_map/all_to_all | solution.py:110
  183.4 2.7 %fusion.52 = bf16[1,1024,1024]{2,1,0:T(8,128)(2,1)S(1)} fusion(bf16[32,16,1024]{2,1,0:T(8,128)(2,1)} %copy-done.17, bf16[32,2,16,1024]{3,2,1,0:T(8,128)(2,1)S(1)} %bitcast.222), kind=kOutput, calls=%fused_computation.81 | convolution fusion | flops 1074790400 | bytes 4194304 | tf_op jit(solution)/shard_map/scd,scf->df/dot_general | solution.py:95
  190.4 3.7 %pad_maximum_fusion.1 = (bf16[2,1024,1024]{2,1,0:T(8,128)(2,1)}, bf16[2,1024,1024]{2,1,0:T(8,128)(2,1)}) fusion(bf16[1,1024,1024]{2,1,0:T(8,128)(2,1)S(1)} %copy-done.4, bf16[1,1024,1024]{2,1,0:T(8,128)(2,1)S(1)} %copy-done.5, bf16[1,1024,1024]{2,1,0:T(8,128)(2,1)S(1)} %copy-done.6, bf16[1,1024,1024]{2,1,0:T(8,128)(2,1)S(1)} %fusion.52), kind=kLoop, calls=%fused_computation.3 | loop fusion | flops 4194304 | bytes 16777216 | tf_op jit(solution)/shard_map/stack | solution.py:117
  197.4 2.8 %all-to-all-done.3 = f32[32,2,16,256]{3,2,1,0:T(8,128)S(1)} async-done(((f32[32,2,16,256]{3,2,1,0:T(8,128)}), f32[32,2,16,256]{3,2,1,0:T(8,128)S(1)}, u32[]{:S(2)}, u32[]{:S(2)}) %all-to-all-start.3) | async-done | bytes 1048608 | tf_op jit(solution)/shard_map/all_to_all | solution.py:110
  (105 shorter events, 43.9 us)
Async XLA Ops:
  7.2 3.1 %copy-start = (bf16[256,2]{0,1:T(2,128)(2,1)S(1)}, bf16[256,2]{0,1:T(2,128)(2,1)}, u32[]{:S(2)}) copy-start(bf16[256,2]{0,1:T(2,128)(2,1)} %param.9) | copy-start | bytes 3076
  7.2 14.1 %copy-start.9 = (bf16[256,256]{1,0:T(8,128)(2,1)S(1)}, bf16[256,256]{1,0:T(8,128)(2,1)}, u32[]{:S(2)}) copy-start(bf16[256,256]{1,0:T(8,128)(2,1)} %param.7) | copy-start | bytes 393220
  11.4 23.0 %all-to-all-start = ((bf16[32,1,32]{2,1,0:T(2,128)(2,1)}), bf16[32,1,32]{2,1,0:T(2,128)(2,1)S(1)}, u32[]{:S(2)}, u32[]{:S(2)}) async-start(bf16[32,1,32]{2,1,0:T(2,128)(2,1)} %all_to_all.24), calls=%async_computation | async-start | bytes 32768 | tf_op jit(solution)/shard_map/all_to_all | solution.py:49
  34.4 9.7 %copy-start.10 = (bf16[256,256]{1,0:T(8,128)(2,1)S(1)}, bf16[256,256]{1,0:T(8,128)(2,1)}, u32[]{:S(2)}) copy-start(bf16[256,256]{1,0:T(8,128)(2,1)} %param.8) | copy-start | bytes 393220
  34.5 38.1 %all-to-all-start.2 = ((bf16[32,32,1024]{2,1,0:T(8,128)(2,1)}), bf16[32,32,1024]{2,1,0:T(8,128)(2,1)S(1)}, u32[]{:S(2)}, u32[]{:S(2)}) async-start(bf16[32,32,1024]{2,1,0:T(8,128)(2,1)} %bitcast.10), calls=%async_computation.2 | async-start | bytes 4194304 | tf_op jit(solution)/shard_map/all_to_all | solution.py:47
  72.5 33.7 %all-to-all-start.1 = ((bf16[32,32,1024]{2,1,0:T(8,128)(2,1)}), bf16[32,32,1024]{2,1,0:T(8,128)(2,1)}, u32[]{:S(2)}, u32[]{:S(2)}) async-start(bf16[32,32,1024]{2,1,0:T(8,128)(2,1)} %bitcast.5), calls=%async_computation.1 | async-start | bytes 4194304 | tf_op jit(solution)/shard_map/all_to_all | solution.py:48
  77.7 95.5 %reduce-scatter.2.cloned.1.call-start = ((), (), s32[]{:S(2)}) async-start(), calls=%async_computation.6 | async-start | bytes 5242880 | tf_op jit(solution)/shard_map/reduce_scatter | solution.py:109
  78.9 4.4 %copy-start.12 = (bf16[2,1024,1024]{2,1,0:T(8,128)(2,1)S(1)}, bf16[2,1024,1024]{2,1,0:T(8,128)(2,1)}, u32[]{:S(2)}) copy-start(bf16[2,1024,1024]{2,1,0:T(8,128)(2,1)} %param.11) | copy-start | bytes 12582916
  106.2 3.4 %copy-start.14 = (bf16[2,1024,1024]{2,1,0:T(8,128)(2,1)S(1)}, bf16[2,1024,1024]{2,1,0:T(8,128)(2,1)}, u32[]{:S(2)}) copy-start(bf16[2,1024,1024]{2,1,0:T(8,128)(2,1)} %param.12) | copy-start | bytes 12582916
  106.2 3.8 %copy-start.21 = (f32[32,16,1024]{2,1,0:T(8,128)S(1)}, f32[32,16,1024]{2,1,0:T(8,128)}, u32[]{:S(2)}) copy-start(f32[32,16,1024]{2,1,0:T(8,128)} %fusion.12) | copy-start | bytes 6291460
  113.0 9.6 %copy-start.18 = (bf16[32,16,1024]{2,1,0:T(8,128)(2,1)}, bf16[32,16,1024]{2,1,0:T(8,128)(2,1)S(1)}, u32[]{:S(2)}) copy-start(bf16[32,16,1024]{2,1,0:T(8,128)(2,1)S(1)} %get-tuple-element.27) | copy-start | bytes 3145732
  128.0 3.7 %copy-start.16 = (bf16[2,1024,1024]{2,1,0:T(8,128)(2,1)S(1)}, bf16[2,1024,1024]{2,1,0:T(8,128)(2,1)}, u32[]{:S(2)}) copy-start(bf16[2,1024,1024]{2,1,0:T(8,128)(2,1)} %param.13) | copy-start | bytes 12582916
  128.0 3.7 %copy-start.25 = (bf16[32,16,1024]{2,1,0:T(8,128)(2,1)S(1)}, bf16[32,16,1024]{2,1,0:T(8,128)(2,1)}, u32[]{:S(2)}) copy-start(bf16[32,16,1024]{2,1,0:T(8,128)(2,1)} %get-tuple-element.22) | copy-start | bytes 3145732
  131.7 4.5 %copy-start.24 = (bf16[32,16,1024]{2,1,0:T(8,128)(2,1)S(1)}, bf16[32,16,1024]{2,1,0:T(8,128)(2,1)}, u32[]{:S(2)}) copy-start(bf16[32,16,1024]{2,1,0:T(8,128)(2,1)} %get-tuple-element.25) | copy-start | bytes 3145732
  134.5 12.2 %collective-permute-start = (f32[32,2,16]{2,1,0:T(2,128)S(1)}, f32[32,2,16]{2,1,0:T(2,128)S(1)}, u32[]{:S(2)}, u32[]{:S(2)}) collective-permute-start(f32[32,2,16]{2,1,0:T(2,128)S(1)} %pad_maximum_fusion.4), channel_id=1, source_target_pairs={{0,1},{1,0},{2,3},{3,2},{4,5},{5,4},{6,7},{7,6},{8,9},{9,8},{10,11... | collective-permute-start | bytes 12296 | tf_op jit(solution)/shard_map/ppermute | solution.py:11
  144.0 5.2 %copy-start.23 = (bf16[32,16,1024]{2,1,0:T(8,128)(2,1)S(1)}, bf16[32,16,1024]{2,1,0:T(8,128)(2,1)}, u32[]{:S(2)}) copy-start(bf16[32,16,1024]{2,1,0:T(8,128)(2,1)} %copy-done.22) | copy-start | bytes 3145732
  146.7 11.6 %copy-start.19 = (bf16[32,16,1024]{2,1,0:T(8,128)(2,1)S(1)}, bf16[32,16,1024]{2,1,0:T(8,128)(2,1)}, u32[]{:S(2)}) copy-start(bf16[32,16,1024]{2,1,0:T(8,128)(2,1)} %copy-done.18) | copy-start | bytes 3145732
  146.7 5.2 %collective-permute-start.1 = (f32[32,2,16]{2,1,0:T(2,128)S(1)}, f32[32,2,16]{2,1,0:T(2,128)S(1)}, u32[]{:S(2)}, u32[]{:S(2)}) collective-permute-start(f32[32,2,16]{2,1,0:T(2,128)S(1)} %fusion.84), channel_id=1, source_target_pairs={{0,2},{1,3},{2,0},{3,1},{4,6},{5,7},{6,4},{7,5},{8,10},{9,11},{10,... | collective-permute-start | bytes 12296 | tf_op jit(solution)/shard_map/ppermute | solution.py:11
  152.5 23.0 %all-to-all-start.4 = ((f32[32,2,16]{2,1,0:T(2,128)}), f32[32,2,16]{2,1,0:T(2,128)S(1)}, u32[]{:S(2)}, u32[]{:S(2)}) async-start(f32[32,2,16]{2,1,0:T(2,128)} %fusion.101), calls=%async_computation.5 | async-start | bytes 65536 | tf_op jit(solution)/shard_map/all_to_all | solution.py:106
  175.6 24.7 %all-to-all-start.3 = ((f32[32,2,16,256]{3,2,1,0:T(8,128)}), f32[32,2,16,256]{3,2,1,0:T(8,128)S(1)}, u32[]{:S(2)}, u32[]{:S(2)}) async-start(f32[32,2,16,256]{3,2,1,0:T(8,128)} %copy.82), calls=%async_computation.4 | async-start | bytes 2097152 | tf_op jit(solution)/shard_map/all_to_all | solution.py:110
  186.1 3.7 %copy-start.5 = (bf16[1,1024,1024]{2,1,0:T(8,128)(2,1)S(1)}, bf16[1,1024,1024]{2,1,0:T(8,128)(2,1)}, u32[]{:S(2)}) copy-start(bf16[1,1024,1024]{2,1,0:T(8,128)(2,1)} %fusion.50) | copy-start | bytes 6291460
  186.1 4.4 %copy-start.6 = (bf16[1,1024,1024]{2,1,0:T(8,128)(2,1)S(1)}, bf16[1,1024,1024]{2,1,0:T(8,128)(2,1)}, u32[]{:S(2)}) copy-start(bf16[1,1024,1024]{2,1,0:T(8,128)(2,1)} %fusion.53) | copy-start | bytes 6291460
  190.4 3.8 %copy-start.11 = (s32[1024]{0:T(1024)S(1)}, s32[1024]{0:T(1024)}, u32[]{:S(2)}) copy-start(s32[1024]{0:T(1024)} %pad_clamp_fusion) | copy-start | bytes 12292
  200.2 4.0 %copy-start.1 = (bf16[256,2]{0,1:T(2,128)(2,1)S(1)}, bf16[256,2]{0,1:T(2,128)(2,1)}, u32[]{:S(2)}) copy-start(bf16[256,2]{0,1:T(2,128)(2,1)} %param.9) | copy-start | bytes 3076
  (10 other events, 23.9 us)
Sparse Core Ops, SparseCore 0:
  128.1 45.0 reduce-scatter.1
